TPU v7x, 256 devices: a whole 4x4x8 slice. The times are simulated.
256 devices in a mesh: fsdp: 16 (over z_hi, x, core), dp: 16 (over z_lo, y).
Axes of the slice: x: 4, y: 4, z: 8 (z_hi: 2, z_lo: 4; z = z_hi * 4 + z_lo), core: 2. Of those that a mesh axis runs over, the one named last changes fastest.
Arguments:
- x_pre: bfloat16 [32768, 4096], P(('fsdp', 'dp')), may hold values from -6 to 6
- x_dec: bfloat16 [1024, 4096], P(('fsdp', 'dp')), may hold values from -6 to 6
- rec_hidden: bfloat16 [81920, 4096], P(('fsdp', 'dp')), may hold values from -6 to 6
- norm_gain: bfloat16 [4096], replicated, may hold values from 0.099609375 to 1.8984375
- w_query: bfloat16 [4096, 2048], P(('fsdp', 'dp')), may hold values from -1 to 1
- key_value_weight: bfloat16 [4096, 512], P(('fsdp', 'dp')), may hold values from -0.09375 to 0.09375
- cache_pool: bfloat16 [21504, 64, 512], P(('fsdp', 'dp')), may hold values from -12 to 12
- shared_kv: bfloat16 [131072, 512], P(('fsdp', 'dp')), may hold values from -12 to 12
- dec_len: int32 [256, 4], P(('fsdp', 'dp')), may hold values from 1 to 3072, as said below
- dec_table: int32 [256, 4, 48], P(('fsdp', 'dp')), may hold values from 0 to 83, as said below
- dec_group: int32 [256, 4], P(('fsdp', 'dp')), may hold values from 0 to 15, as said below
- prefix_len: int32 [16, 16], P('fsdp'), may hold values from 1 to 512, as said below
- pre_start: int32 [256], P(('fsdp', 'dp')), may hold values from 0 to 1024, as said below
- pre_table: int32 [256, 16], P(('fsdp', 'dp')), may hold values from 0 to 83, as said below
- rec_req: int32 [256, 320], P(('fsdp', 'dp')), may hold values from 0 to 3, as said below
- rec_off: int32 [256, 320], P(('fsdp', 'dp')), may hold values from 0 to 3071, as said below
Outputs:
- out_pre: bfloat16 [32768, 2048], P(('fsdp', 'dp'))
- out_dec: bfloat16 [1024, 2048], P(('fsdp', 'dp'))
Inputs may be any that keep to these rules, and one draw needn't show every extreme that they name: `dec_len`: the private lengths of one device's decode requests sum to 4096; each device has one request of length exactly 3072. `dec_table`: the pages of one device's decode requests (the first ceil(dec_len / 64) entries of each row) and of its prefill history (the first pre_start / 64 entries) are all different; later entries are valid page numbers. `pre_table`: same pages as stated for dec_table. `dec_group`: A group names a device with the same fsdp index; a few groups along a line are far more common than the others. `prefix_len`: in every fsdp line some device holds a prefix of length exactly 512. `pre_start`: A multiple of 64; some device starts at exactly 1024. `rec_req`: the recomputed tokens of one device are different tokens of its decode requests. `rec_off`: below the request's dec_len.
All inputs are finite; a program needn't handle non-finite values.
Results may differ from a plain program's by a relative error of at most 0.0073.
Values may be sent and summed in bfloat16 or wider, within the bound.
No kernel may reach another device: no remote copies, remote signals or barrier semaphores. Data moves between devices by JAX's collectives and lax.ppermute only.
A program may use at most 192 MiB of HBM per device.

v0:
```python
import jax
import jax.numpy as jnp
from jax import lax
from jax.sharding import PartitionSpec as P

QUERY_HEADS = 16
KEY_VALUE_HEADS = 2
HEAD_SIZE = 128
PAGE_TOKENS = 64
theta_base = 5000000.0
epsilon = 1e-05
negative_large = -1e30


def rms_scaled(values, gain):
    widened = values.astype(jnp.float32)
    factor = lax.rsqrt(jnp.mean(widened * widened, axis=-1, keepdims=True) + epsilon)
    return (widened * factor * gain.astype(jnp.float32)).astype(jnp.bfloat16)


def rotate_halves(vectors, positions):
    half_dim = vectors.shape[-1] // 2
    frequency = theta_base ** (-jnp.arange(half_dim, dtype=jnp.float32) * 2.0 / vectors.shape[-1])
    angles = positions.astype(jnp.float32)[:, None, None] * frequency
    cosines = jnp.cos(angles)
    sines = jnp.sin(angles)
    first_half = vectors[..., :half_dim]
    second_half = vectors[..., half_dim:]
    return jnp.concatenate(
        [first_half * cosines - second_half * sines, second_half * cosines + first_half * sines],
        axis=-1,
    )


def small_lookup(entries, indices):
    matches = indices[..., None] == jnp.arange(entries.shape[0], dtype=jnp.int32)
    return jnp.sum(jnp.where(matches, entries, 0), axis=-1)


def attend_portion(query, keys, values, visible_mask, per_request):
    if per_request:
        score_form = "qojv,qeov->qoje"
        value_form = "wucm,wmuf->wucf"
    else:
        score_form = "rkgd,tkd->rkgt"
        value_form = "rkgt,tkd->rkgd"
    score_matrix = jnp.einsum(
        score_form, query, keys, preferred_element_type=jnp.float32
    ) * query.shape[-1] ** (-0.5)
    allowed = visible_mask[:, None, None, :]
    masked = jnp.where(allowed, score_matrix, negative_large)
    maxima = jnp.max(masked, axis=-1)
    weight_matrix = jnp.where(allowed, jnp.exp(masked - maxima[..., None]), 0.0)
    totals = jnp.sum(weight_matrix, axis=-1)
    summed_output = jnp.einsum(
        value_form, weight_matrix, values.astype(jnp.float32), precision=lax.Precision.HIGHEST
    )
    return (maxima, totals, summed_output)


def combine(first_part, second_part):
    maxima = jnp.maximum(first_part[0], second_part[0])
    left_scale = jnp.exp(first_part[0] - maxima)
    right_scale = jnp.exp(second_part[0] - maxima)
    totals = first_part[1] * left_scale + second_part[1] * right_scale
    summed_output = first_part[2] * left_scale[..., None] + second_part[2] * right_scale[..., None]
    return (maxima, totals, summed_output)


def on_device(
    x_pre,
    x_dec,
    rec_hidden,
    norm_gain,
    w_query,
    key_value_weight,
    cache_pool,
    shared_kv,
    dec_len,
    dec_table,
    dec_group,
    prefix_len,
    pre_start,
    pre_table,
    rec_req,
    rec_off,
):
    group_share = QUERY_HEADS // KEY_VALUE_HEADS
    key_value_width = KEY_VALUE_HEADS * HEAD_SIZE
    prefill_count = x_pre.shape[0]
    decode_count = x_dec.shape[0]
    lengths = dec_len[0]
    page_table = dec_table[0]
    groups = dec_group[0]
    prefix_line = prefix_len[0]
    request = rec_req[0]
    within = rec_off[0]
    query_rows = jnp.concatenate(
        [rms_scaled(x_pre, norm_gain), rms_scaled(x_dec, norm_gain)], axis=0
    )
    key_value_rows = jnp.concatenate([query_rows, rms_scaled(rec_hidden, norm_gain)], axis=0)
    whole_query, whole_keyval = (
        lax.all_gather(w_query, ("fsdp", "dp"), axis=0, tiled=True),
        lax.all_gather(key_value_weight, ("fsdp", "dp"), axis=0, tiled=True),
    )
    query_proj = jnp.dot(query_rows, whole_query, preferred_element_type=jnp.float32)
    key_value_projected = jnp.dot(key_value_rows, whole_keyval, preferred_element_type=jnp.float32)
    pre_pos = pre_start[0] + jnp.arange(prefill_count, dtype=jnp.int32)
    dec_pos = small_lookup(prefix_line, groups) + lengths
    rec_pos = small_lookup(prefix_line, small_lookup(groups, request)) + within
    query_pos = jnp.concatenate([pre_pos, dec_pos], axis=0)
    query_matrix = rotate_halves(query_proj.reshape(-1, QUERY_HEADS, HEAD_SIZE), query_pos).astype(
        jnp.bfloat16
    )
    key_value_positions = jnp.concatenate([query_pos, rec_pos], axis=0)
    key_value_heads = key_value_projected.reshape(-1, 2 * KEY_VALUE_HEADS, HEAD_SIZE)
    new_key_value = jnp.concatenate(
        [
            rotate_halves(key_value_heads[:, :KEY_VALUE_HEADS], key_value_positions),
            key_value_heads[:, KEY_VALUE_HEADS:],
        ],
        axis=1,
    ).astype(jnp.bfloat16)
    added_rows = new_key_value.reshape(-1, 2 * key_value_width)
    max_pages = page_table.shape[1]
    rec_page = page_table.reshape(-1)[request * max_pages + within // PAGE_TOKENS]
    flattened_pool = cache_pool.reshape(-1, 2 * key_value_width)
    flattened_pool = flattened_pool.at[rec_page * PAGE_TOKENS + within % PAGE_TOKENS].set(
        added_rows[prefill_count + decode_count :]
    )
    slot_range = jnp.arange(PAGE_TOKENS, dtype=jnp.int32)
    private_lookup = (page_table[:, :, None] * PAGE_TOKENS + slot_range).reshape(decode_count, -1)
    private_keys = flattened_pool[private_lookup].reshape(
        decode_count, -1, 2 * KEY_VALUE_HEADS, HEAD_SIZE
    )
    private_seen = jnp.arange(private_keys.shape[1], dtype=jnp.int32)[None, :] < lengths[:, None]
    decode_query = query_matrix[prefill_count:].reshape(
        decode_count, KEY_VALUE_HEADS, group_share, HEAD_SIZE
    )
    private_part = attend_portion(
        decode_query,
        private_keys[:, :, :KEY_VALUE_HEADS],
        private_keys[:, :, KEY_VALUE_HEADS:],
        private_seen,
        True,
    )
    fresh_keys = new_key_value[prefill_count : prefill_count + decode_count][:, None]
    fresh_part = attend_portion(
        decode_query,
        fresh_keys[:, :, :KEY_VALUE_HEADS],
        fresh_keys[:, :, KEY_VALUE_HEADS:],
        jnp.ones((decode_count, 1), dtype=bool),
        True,
    )
    local_part = combine(private_part, fresh_part)
    span = shared_kv.shape[0]
    start_portion = (
        jnp.full((decode_count, KEY_VALUE_HEADS, group_share), negative_large, jnp.float32),
        jnp.zeros((decode_count, KEY_VALUE_HEADS, group_share), jnp.float32),
        jnp.zeros((decode_count, KEY_VALUE_HEADS, group_share, HEAD_SIZE), jnp.float32),
    )
    slice_portion = lax.all_gather(shared_kv, "dp", axis=0, tiled=True)
    row_counter = slice_portion.shape[0]
    row_ids = jnp.arange(row_counter, dtype=jnp.int32)
    owner_ids = row_ids // span
    limits = small_lookup(prefix_line, owner_ids)
    visible_mask = (owner_ids[None, :] == groups[:, None]) & (row_ids % span < limits)[None, :]
    head_groups = slice_portion.reshape(row_counter, 2 * KEY_VALUE_HEADS, HEAD_SIZE)
    shared_part = combine(
        start_portion,
        attend_portion(
            decode_query,
            head_groups[:, :KEY_VALUE_HEADS],
            head_groups[:, KEY_VALUE_HEADS:],
            visible_mask,
            False,
        ),
    )
    final_part = combine(local_part, shared_part)
    out_dec = (
        (final_part[2] / final_part[1][..., None])
        .astype(jnp.bfloat16)
        .reshape(decode_count, QUERY_HEADS * HEAD_SIZE)
    )
    history_lookup = (pre_table[0][:, None] * PAGE_TOKENS + slot_range).reshape(-1)
    cached_count = history_lookup.shape[0]
    prefill_context = jnp.concatenate(
        [flattened_pool[history_lookup], added_rows[:prefill_count]], axis=0
    ).reshape(-1, 2 * KEY_VALUE_HEADS, HEAD_SIZE)
    row_ids = jnp.arange(prefill_count, dtype=jnp.int32)
    pre_visible = jnp.concatenate(
        [
            jnp.broadcast_to(
                jnp.arange(cached_count, dtype=jnp.int32)[None, :] < pre_start[0],
                (prefill_count, cached_count),
            ),
            row_ids[None, :] <= row_ids[:, None],
        ],
        axis=1,
    )
    prefill_query = query_matrix[:prefill_count].reshape(
        prefill_count, KEY_VALUE_HEADS, group_share, HEAD_SIZE
    )
    prefill_scores = jnp.einsum(
        "uwvm,owm->wvuo",
        prefill_query,
        prefill_context[:, :KEY_VALUE_HEADS],
        preferred_element_type=jnp.float32,
    ) * HEAD_SIZE ** (-0.5)
    pre_allowed = pre_visible[None, None]
    pre_masked = jnp.where(pre_allowed, prefill_scores, negative_large)
    pre_max = jnp.max(pre_masked, axis=-1, keepdims=True)
    pre_weights = jnp.where(pre_allowed, jnp.exp(pre_masked - pre_max), 0.0)
    prefill_probabilities = (pre_weights / jnp.sum(pre_weights, axis=-1, keepdims=True)).astype(
        jnp.bfloat16
    )
    out_pre = jnp.einsum(
        "jcse,eji->sjci",
        prefill_probabilities,
        prefill_context[:, KEY_VALUE_HEADS:],
        preferred_element_type=jnp.float32,
    )
    return (out_pre.astype(jnp.bfloat16).reshape(prefill_count, QUERY_HEADS * HEAD_SIZE), out_dec)


def solution(mesh):
    return jax.shard_map(
        on_device,
        mesh=mesh,
        in_specs=(
            P(("fsdp", "dp"), None),
            P(("fsdp", "dp"), None),
            P(("fsdp", "dp"), None),
            P(),
            P(("fsdp", "dp"), None),
            P(("fsdp", "dp"), None),
            P(("fsdp", "dp"), None, None),
            P(("fsdp", "dp"), None),
            P(("fsdp", "dp"), None),
            P(("fsdp", "dp"), None, None),
            P(("fsdp", "dp"), None),
            P("fsdp", None),
            P(("fsdp", "dp")),
            P(("fsdp", "dp"), None),
            P(("fsdp", "dp"), None),
            P(("fsdp", "dp"), None),
        ),
        out_specs=(P(("fsdp", "dp"), None), P(("fsdp", "dp"), None)),
        check_vma=False,
    )
```

profile of v0, /device:TPU:1, one launch (start us, length us, event | category | flops | bytes accessed | tf_op | source)
XLA Modules:
  0.0 1581.3 jit_solution(894209553763811438)
XLA Ops:
  7.3 5.7 copy.216
  13.1 0.7 all-gather.6.cloned.1.call-update
  13.9 1.0 copy.125
  15.1 0.1 reshape_squeeze.3
  15.9 0.1 fusion.90
  16.0 0.2 select_reduce_fusion.3
  16.2 0.1 select_reduce_fusion.2
  16.3 0.1 select_reduce_fusion.1
  16.5 0.1 add_convert_fusion.2
  16.5 2.4 gather_fusion
  19.0 0.6 fusion.114
  19.6 0.1 iota_add_fusion
  19.6 0.1 add.263
  19.7 0.2 select_reduce_fusion
  19.9 0.1 add.267
  20.0 0.1 add.268
  20.3 1.6 fusion.28
  21.9 0.6 fusion.8
  22.6 0.3 multiply_cosine_fusion.1
  22.9 0.9 multiply_cosine_fusion
  23.8 0.9 pad_add_fusion
  24.7 0.7 iota_compare_fusion.2
  25.4 0.1 fusion.92
  25.5 1.3 fusion.30
  26.8 2.3 fusion.10
  29.1 0.1 compare_and_fusion
  29.2 695.2 %all-gather.4.cloned.1.call-done = bf16[4096,512]{1,0:T(8,128)(2,1)} async-done(((bf16[16,512]{1,0:T(8,128)(2,1)}), bf16[4096,512]{1,0:T(8,128)(2,1)}) %all-gather.4.cloned.1.call-update) | async-done | bytes 4194320 | tf_op jit(solution)/shard_map/all_gather | solution.py:104
  724.4 5.4 fusion.16
  729.8 0.3 reshape.640
  730.1 0.2 slice.145
  730.4 0.7 subtract_convert_fusion.1
  731.1 0.3 pad_maximum_fusion.2
  731.4 0.7 copy.119
  732.1 0.9 pad_maximum_fusion.1
  733.0 0.1 slice.90
  733.1 7.9 scatter_custom_fusion
  741.1 7.3 gather_fusion.1
  748.3 0.5 copy.117
  748.9 1.3 copy.118
  750.2 53.4 %gather_fusion.2 = bf16[12288,512]{1,0:T(8,128)(2,1)} fusion(bf16[5376,512]{1,0:T(8,128)(2,1)} %scatter_custom_fusion, s32[12288]{0:T(1024)S(1)} %broadcast_clamp_fusion), kind=kCustom, calls=%fused_computation.2 | custom fusion | bytes 25214976 | tf_op jit(solution)/shard_map/gather | solution.py:133
  803.6 18.2 %reshape.645 = bf16[4,3072,4,128]{3,2,1,0:T(4,128)(2,1)} reshape(bf16[12288,512]{1,0:T(8,128)(2,1)} %gather_fusion.2) | data formatting | bytes 25165824 | tf_op jit(solution)/shard_map/reshape | solution.py:133
  821.8 0.1 maximum_bitcast_fusion
  821.9 16.0 %fusion.127 = (bf16[4,3072,2,128]{3,2,1,0:T(2,128)(2,1)}, bf16[4,3072,2,128]{3,2,1,0:T(2,128)(2,1)}) fusion(bf16[4,3072,4,128]{3,2,1,0:T(4,128)(2,1)} %reshape.645), kind=kLoop, calls=%fused_computation.182 | loop fusion | bytes 25165824 | tf_op jit(solution)/shard_map/slice | solution.py:143
  838.0 618.8 %all-gather.6.cloned.1.call-done = bf16[4096,2048]{1,0:T(8,128)(2,1)} async-done(((bf16[16,2048]{1,0:T(8,128)(2,1)}), bf16[4096,2048]{1,0:T(8,128)(2,1)}) %all-gather.6.cloned.1.call-update) | async-done | bytes 16777232 | tf_op jit(solution)/shard_map/all_gather | solution.py:103
  1456.7 8.2 fusion.35
  1465.0 0.2 copy.147
  1465.3 0.6 add_convert_fusion
  1465.9 0.3 fusion.77
  1466.2 0.1 copy.120
  1466.3 0.1 copy-done.4
  1466.5 6.5 fusion.128
  1472.9 4.7 fusion.34
  1477.6 1.0 copy.133
  1478.6 0.1 fusion.102
  1478.7 0.1 fusion.109
  1478.8 81.8 %all-gather.8.cloned.1.call-done = bf16[8192,512]{0,1:T(8,128)(2,1)} async-done(((bf16[512,512]{0,1:T(8,128)(2,1)}), bf16[8192,512]{0,1:T(8,128)(2,1)}) %all-gather.8.cloned.1.call-update) | async-done | bytes 8388624 | tf_op jit(solution)/shard_map/all_gather | solution.py:162
  1560.6 3.3 fusion.131
  1563.9 0.7 fusion.126
  1564.7 1.8 fusion.132
  1566.5 0.3 fusion.72
  1566.9 0.5 copy-done.3
  1567.4 4.0 fusion.48
  1571.4 2.7 fusion.69
  1574.1 0.6 copy.212
  (82 shorter events, 0.7 us)
Async XLA Ops:
  7.2 8.7 copy-start.11
  7.2 8.7 copy-start.8
  7.2 6.7 copy-start.5
  7.2 9.2 copy-start.17
  7.2 7.9 copy-start.12
  7.2 8.8 copy-start.15
  7.2 8.8 copy-start.14
  7.2 12.3 copy-start.18
  7.2 7.7 copy-start.13
  7.3 7.7 copy-start.10
  7.3 717.1 %all-gather.4.cloned.1.call-start = ((), (), s32[]{:S(2)}) async-start(), calls=%async_computation | async-start | bytes 4210688 | tf_op jit(solution)/shard_map/all_gather | solution.py:104
  13.1 8.8 copy-start
  13.1 1443.7 %all-gather.6.cloned.1.call-start = ((), (), s32[]{:S(2)}) async-start(), calls=%async_computation.1 | async-start | bytes 16842752 | tf_op jit(solution)/shard_map/all_gather | solution.py:103
  13.8 1546.8 %all-gather.8.cloned.1.call-start = ((), (), s32[]{:S(2)}) async-start(), calls=%async_computation.2 | async-start | bytes 8912896 | tf_op jit(solution)/shard_map/all_gather | solution.py:162
  20.2 5.3 copy-start.2
  22.5 6.6 copy-start.16
  821.9 634.8 %copy-start.1 = (bf16[128,4096]{1,0:T(8,128)(2,1)S(1)}, bf16[128,4096]{1,0:T(8,128)(2,1)}, u32[]{:S(2)}) copy-start(bf16[128,4096]{1,0:T(8,128)(2,1)} %fusion.30) | copy-start | bytes 3145732
  1465.2 1.2 copy-start.4
  1465.2 1.2 copy-start.6
  1465.2 1.2 copy-start.7
  1478.6 86.1 %slice-start = ((s8[6291456]{0:T(1024)(128)(4,1)}), s8[2097152]{0:T(1024)(128)(4,1)S(1)}, s32[]{:S(2)}) async-start(s8[6291456]{0:T(1024)(128)(4,1)} %bitcast.130), calls=%async_computation.3 | async-start | bytes 4194304
  1560.6 4.0 slice-start.1
  1560.6 4.0 copy-start.9
  1563.9 3.4 copy-start.3
  1564.7 6.7 slice-start.2
  1566.9 4.6 slice-start.3
Sparse Core Ops, SparseCore 0:
  13.2 711.1 all-gather.3
  726.2 730.4 all-gather.5
  1458.5 102.0 all-gather.7
where the time goes:
time: 1580 us
  waiting for transfers between devices  1400 us (89%)
  local copies, waits for them, and re-layouts  118 us (7%)
  matrix products  36.7 us (2%)
    all_gather x1, waiting for transfers between devices, on_device(): lax.all_gather(key_value_weight, ('fsdp', 'dp'), axis=0, tiled=True)  695 us
    all_gather x1, waiting for transfers between devices, on_device(): lax.all_gather(w_query, ('fsdp', 'dp'), axis=0, tiled=True)  619 us
    all_gather x1, waiting for transfers between devices, on_device(): slice_portion = lax.all_gather(shared_kv, 'dp', axis=0, tiled=True)  81.8 us
    gather x1, local copies, waits for them, and re-layouts, on_device(): flattened_pool[private_lookup]  53.4 us
  transfers between devices with their start and end apart: 3, of which 3 were waited for; matrix products, arithmetic and copies ran while one was open for 9% of the time, Pallas kernels for 0%

commit v1 on v0

--- a/solution.py
+++ b/solution.py
@@ -101,7 +101,12 @@
     key_value_rows = jnp.concatenate([query_rows, rms_scaled(rec_hidden, norm_gain)], axis=0)
     whole_query, whole_keyval = (
         lax.all_gather(w_query, ("fsdp", "dp"), axis=0, tiled=True),
-        lax.all_gather(key_value_weight, ("fsdp", "dp"), axis=0, tiled=True),
+        jnp.concatenate(
+            lax.all_to_all(
+                jnp.stack([key_value_weight] * lax.axis_size(("fsdp", "dp"))), ("fsdp", "dp"), 0, 0
+            ),
+            axis=0,
+        ),
     )
     query_proj = jnp.dot(query_rows, whole_query, preferred_element_type=jnp.float32)
     key_value_projected = jnp.dot(key_value_rows, whole_keyval, preferred_element_type=jnp.float32)

time: 1580 us -> 905 us (0.57)
  waiting for transfers between devices: 1400 us -> 689 us
  starting transfers between devices: 0.12 us -> 16.7 us
    all_gather x1 -> x0, waiting for transfers between devices: 695 us -> none  [on_device(): lax.all_gather(key_value_weight, ('fsdp', 'dp'), axis=0, tiled=True)]
    all_gather x1, waiting for transfers between devices: 619 us -> 518 us  [on_device(): lax.all_gather(w_query, ('fsdp', 'dp'), axis=0, tiled=True)]
    all_to_all x0 -> x1, waiting for transfers between devices: none -> 85.9 us  [on_device(): lax.all_to_all(jnp.stack([key_value_weight] * lax.axis_size(('fsdp', 'dp'...]
    all_to_all x0 -> x1, starting transfers between devices: none -> 16.7 us  [on_device(): lax.all_to_all(jnp.stack([key_value_weight] * lax.axis_size(('fsdp', 'dp'...]
  transfers between devices with their start and end apart: 3 -> 3, of which waited for: 3 -> 3; matrix products, arithmetic and copies ran while one was open for 9% -> 18% of each run, Pallas kernels for 0% -> 0%
where the time goes in v1:
time: 905 us; the launch traced here: 903 us
  waiting for transfers between devices  689 us (76%)
  local copies, waits for them, and re-layouts  130 us (14%)
  matrix products  36.1 us (4%)
  starting transfers between devices  16.7 us (2%)
  between operations  15.3 us (2%)
  other arithmetic  15.2 us (2%)
    all_gather x1, waiting for transfers between devices, on_device(): lax.all_gather(w_query, ('fsdp', 'dp'), axis=0, tiled=True)  518 us
    all_to_all x1, waiting for transfers between devices, on_device(): lax.all_to_all(jnp.stack([key_value_weight] * lax.axis_size(('fsdp', 'dp'...  85.9 us
    all_gather x1, waiting for transfers between devices, on_device(): slice_portion = lax.all_gather(shared_kv, 'dp', axis=0, tiled=True)  85.4 us
    gather x1, local copies, waits for them, and re-layouts, on_device(): flattened_pool[private_lookup]  57.3 us
    reshape x1, local copies, waits for them, and re-layouts, on_device(): flattened_pool[private_lookup]  18.2 us
  transfers between devices with their start and end apart: 3, of which 3 were waited for; matrix products, arithmetic and copies ran while one was open for 18% of the time, Pallas kernels for 0%

profile of v1, /device:TPU:1, one launch (start us, length us, event | category | flops | bytes accessed | tf_op | source)
XLA Modules:
  0.0 902.7 jit_solution(5248746416793368621)
XLA Ops:
  7.2 5.6 copy.189
  12.9 2.6 stack.2
  15.6 16.7 %all-to-all-start = ((bf16[256,16,512]{2,1,0:T(8,128)(2,1)}), bf16[256,16,512]{2,1,0:T(8,128)(2,1)}, u32[]{:S(2)}, u32[]{:S(2)}) async-start(bf16[256,16,512]{2,1,0:T(8,128)(2,1)} %stack.2), calls=%async_computation | async-start | bytes 8388608 | tf_op jit(solution)/shard_map/all_to_all | solution.py:105
  32.4 1.0 copy.98
  33.5 0.1 reshape_squeeze.3
  34.3 0.1 fusion.81
  34.5 1.5 fusion.27
  36.0 0.2 select_reduce_fusion.3
  36.2 0.1 select_reduce_fusion.2
  36.3 0.1 select_reduce_fusion.1
  36.5 2.4 gather_fusion
  39.0 0.6 fusion.105
  39.7 0.1 add.267
  39.8 0.1 add.268
  40.0 0.1 add.263
  40.1 0.2 select_reduce_fusion
  40.3 0.6 fusion.8
  41.0 0.3 multiply_cosine_fusion.1
  41.3 0.9 multiply_cosine_fusion
  42.2 0.6 broadcast_clamp_fusion
  42.8 0.9 pad_add_fusion
  43.7 0.7 iota_compare_fusion.2
  44.4 0.1 fusion.83
  44.5 1.3 fusion.29
  45.8 2.3 fusion.10
  48.2 0.1 compare_and_fusion
  48.3 85.9 %all-to-all-done = bf16[256,16,512]{2,1,0:T(8,128)(2,1)} async-done(((bf16[256,16,512]{2,1,0:T(8,128)(2,1)}), bf16[256,16,512]{2,1,0:T(8,128)(2,1)}, u32[]{:S(2)}, u32[]{:S(2)}) %all-to-all-start) | async-done | bytes 4194336 | tf_op jit(solution)/shard_map/all_to_all | solution.py:105
  134.1 6.5 copy.88
  140.7 5.1 fusion.16
  145.9 0.2 subtract_convert_fusion.1
  146.2 0.1 pad_maximum_fusion.2
  146.3 0.1 slice_bitcast_fusion.20
  146.4 0.2 copy-done.5
  146.6 0.2 copy-done.3
  146.8 7.9 scatter_custom_fusion
  154.8 7.3 gather_fusion.1
  162.1 0.5 copy.90
  162.6 0.7 copy.91
  163.3 57.3 %gather_fusion.2 = bf16[12288,512]{1,0:T(8,128)(2,1)} fusion(bf16[5376,512]{1,0:T(8,128)(2,1)} %scatter_custom_fusion, s32[12288]{0:T(1024)} %broadcast_clamp_fusion), kind=kCustom, calls=%fused_computation.2 | custom fusion | bytes 25214976 | tf_op jit(solution)/shard_map/gather | solution.py:138
  220.6 18.2 %reshape.649 = bf16[4,3072,4,128]{3,2,1,0:T(4,128)(2,1)} reshape(bf16[12288,512]{1,0:T(8,128)(2,1)} %gather_fusion.2) | data formatting | bytes 25165824 | tf_op jit(solution)/shard_map/reshape | solution.py:138
  238.9 0.6 fusion.102
  239.5 1.1 fusion.34
  240.6 16.0 %fusion.114 = (bf16[4,3072,2,128]{3,2,1,0:T(2,128)(2,1)}, bf16[4,3072,2,128]{3,2,1,0:T(2,128)(2,1)}) fusion(bf16[4,3072,4,128]{3,2,1,0:T(4,128)(2,1)} %reshape.649), kind=kLoop, calls=%fused_computation.178 | loop fusion | bytes 25165824 | tf_op jit(solution)/shard_map/slice | solution.py:148
  256.7 518.0 %all-gather.3.cloned.1.call-done = bf16[4096,2048]{1,0:T(8,128)(2,1)} async-done(((bf16[16,2048]{1,0:T(8,128)(2,1)}), bf16[4096,2048]{1,0:T(8,128)(2,1)}) %all-gather.3.cloned.1.call-update) | async-done | bytes 16777232 | tf_op jit(solution)/shard_map/all_gather | solution.py:103
  774.6 8.2 fusion.35
  782.9 0.2 copy.120
  783.2 0.6 add_convert_fusion
  783.7 0.3 fusion.73
  784.0 0.1 copy.92
  784.2 0.2 copy-done.8
  784.3 6.1 fusion.115
  790.4 4.7 fusion.33
  795.1 1.0 copy.106
  796.1 0.1 fusion.93
  796.2 0.1 fusion.100
  796.3 85.4 %all-gather.5.cloned.1.call-done = bf16[8192,512]{0,1:T(8,128)(2,1)} async-done(((bf16[512,512]{0,1:T(8,128)(2,1)}), bf16[8192,512]{0,1:T(8,128)(2,1)}) %all-gather.5.cloned.1.call-update) | async-done | bytes 8388624 | tf_op jit(solution)/shard_map/all_gather | solution.py:167
  881.7 3.3 fusion.116
  885.0 0.7 fusion.113
  885.8 1.8 fusion.117
  887.6 0.3 fusion.72
  888.0 0.5 copy-done.7
  888.4 4.1 fusion.48
  892.5 2.7 fusion.69
  895.2 0.6 copy.185
  (94 shorter events, 0.9 us)
Async XLA Ops:
  7.2 5.7 copy-start.15
  7.2 767.5 %all-gather.3.cloned.1.call-start = ((), (), s32[]{:S(2)}) async-start(), calls=%async_computation.1 | async-start | bytes 16842752 | tf_op jit(solution)/shard_map/all_gather | solution.py:103
  15.5 16.8 %copy-start.9 = (bf16[512,512]{1,0:T(8,128)(2,1)S(1)}, bf16[512,512]{1,0:T(8,128)(2,1)}, u32[]{:S(2)}) copy-start(bf16[512,512]{1,0:T(8,128)(2,1)} %param.23) | copy-start | bytes 1572868
  15.5 17.9 %copy-start.19 = (s32[1,320]{1,0:T(1,128)S(1)}, s32[1,320]{1,0:T(1,128)}, u32[]{:S(2)}) copy-start(s32[1,320]{1,0:T(1,128)} %param.30) | copy-start | bytes 3844
  15.5 17.9 %copy-start.16 = (s32[1,320]{1,0:T(1,128)S(1)}, s32[1,320]{1,0:T(1,128)}, u32[]{:S(2)}) copy-start(s32[1,320]{1,0:T(1,128)} %param.31) | copy-start | bytes 3844
  15.5 18.0 %copy-start.18 = (s32[1,4,48]{2,1,0:T(4,128)S(1)}, s32[1,4,48]{2,1,0:T(4,128)}, u32[]{:S(2)}) copy-start(s32[1,4,48]{2,1,0:T(4,128)} %param.25) | copy-start | bytes 2308
  15.5 18.7 %copy-start.13 = (bf16[4,4096]{1,0:T(4,128)(2,1)S(1)}, bf16[4,4096]{1,0:T(4,128)(2,1)}, u32[]{:S(2)}) copy-start(bf16[4,4096]{1,0:T(4,128)(2,1)} %param.17) | copy-start | bytes 98308
  15.6 20.4 %copy-start.20 = (s32[1,16]{1,0:T(1,128)S(1)}, s32[1,16]{1,0:T(1,128)}, u32[]{:S(2)}) copy-start(s32[1,16]{1,0:T(1,128)} %param.27) | copy-start | bytes 196
  15.6 20.4 %copy-start.21 = (s32[1,4]{1,0:T(1,128)S(1)}, s32[1,4]{1,0:T(1,128)}, u32[]{:S(2)}) copy-start(s32[1,4]{1,0:T(1,128)} %param.26) | copy-start | bytes 52
  15.6 20.8 %copy-start.23 = (s32[1,4]{1,0:T(1,128)S(1)}, s32[1,4]{1,0:T(1,128)}, u32[]{:S(2)}) copy-start(s32[1,4]{1,0:T(1,128)} %param.24) | copy-start | bytes 52
  15.6 118.6 %all-to-all-start = ((bf16[256,16,512]{2,1,0:T(8,128)(2,1)}), bf16[256,16,512]{2,1,0:T(8,128)(2,1)}, u32[]{:S(2)}, u32[]{:S(2)}) async-start(bf16[256,16,512]{2,1,0:T(8,128)(2,1)} %stack.2), calls=%async_computation | async-start | bytes 8388608 | tf_op jit(solution)/shard_map/all_to_all | solution.py:105
  32.3 7.3 copy-start.24
  32.3 7.7 copy-start.17
  32.3 8.0 copy-start
  32.3 849.4 %all-gather.5.cloned.1.call-start = ((), (), s32[]{:S(2)}) async-start(), calls=%async_computation.2 | async-start | bytes 8912896 | tf_op jit(solution)/shard_map/all_gather | solution.py:167
  40.1 4.4 copy-start.2
  44.5 96.2 %copy-start.11 = (bf16[4,4096]{1,0:T(4,128)(2,1)}, bf16[4,4096]{1,0:T(4,128)(2,1)S(1)}, u32[]{:S(2)}) copy-start(bf16[4,4096]{1,0:T(4,128)(2,1)S(1)} %fusion.83) | copy-start | bytes 98308
  134.1 6.6 copy-start.1
  145.9 0.7 copy-start.5
  146.1 0.7 copy-start.3
  220.6 18.2 %copy-start.4 = (bf16[452,2,64]{2,0,1:T(8,128)(2,1)S(1)}, bf16[452,2,64]{2,0,1:T(8,128)(2,1)}, u32[]{:S(2)}) copy-start(bf16[452,2,64]{2,0,1:T(8,128)(2,1)} %copy-done.3) | copy-start | bytes 347140
  220.6 18.2 %copy-start.6 = (bf16[452,2,128]{2,0,1:T(8,128)(2,1)S(1)}, bf16[452,2,128]{2,0,1:T(8,128)(2,1)}, u32[]{:S(2)}) copy-start(bf16[452,2,128]{2,0,1:T(8,128)(2,1)} %copy-done.5) | copy-start | bytes 694276
  240.6 534.0 %copy-start.12 = (bf16[4,4096]{1,0:T(4,128)(2,1)S(1)}, bf16[4,4096]{1,0:T(4,128)(2,1)}, u32[]{:S(2)}) copy-start(bf16[4,4096]{1,0:T(4,128)(2,1)} %copy-done.11) | copy-start | bytes 98308
  783.1 1.3 copy-start.8
  783.1 1.3 copy-start.10
  790.4 5.8 copy-start.22
  796.1 89.6 %slice-start = ((s8[6291456]{0:T(1024)(128)(4,1)}), s8[2097152]{0:T(1024)(128)(4,1)S(1)}, s32[]{:S(2)}) async-start(s8[6291456]{0:T(1024)(128)(4,1)} %bitcast.138), calls=%async_computation.3 | async-start | bytes 4194304
  881.7 4.0 slice-start.1
  881.7 4.0 copy-start.14
  885.0 3.4 copy-start.7
  885.8 6.7 slice-start.2
  887.9 4.6 slice-start.3
Sparse Core Ops, SparseCore 0:
  13.0 761.5 all-gather.2
  776.4 105.2 all-gather.4
